TPU v7x, 512 devices: a whole 4x8x8 slice. The times are simulated.
512 devices in a mesh: dp: 8 (over z), context: 16 (over y, core), tensor: 4 (over x).
Axes of the slice: x: 4, y: 8, z: 8, core: 2. Of those that a mesh axis runs over, the one named last changes fastest.
Arguments:
- layer_input: bfloat16 [8, 8192, 4096], P('dp', 'context', 'tensor'), may hold values from -6 to 6
- queries: bfloat16 [8, 16, 8192, 128], P('dp', 'tensor', 'context'), may hold values from -6 to 6
- key_states: bfloat16 [8, 4, 8192, 128], P('dp', 'tensor', 'context'), may hold values from -6 to 6
- value_states: bfloat16 [8, 4, 8192, 128], P('dp', 'tensor', 'context'), may hold values from -6 to 6
- out_grad: bfloat16 [8, 16, 8192, 128], P('dp', 'tensor', 'context'), may hold values from -0.0234375 to 0.0234375
- log_sums: bfloat16 [8, 16, 8192], P('dp', 'tensor', 'context'), may hold values from 2 to 5
- grad_dots: bfloat16 [8, 16, 8192], P('dp', 'tensor', 'context'), may hold values from -0.1875 to 0.1875
- doc_stretches: int32 [8, 10], P('dp'), may hold values from 1 to 8, as said below
- stretch_order: int32 [8, 256], P('dp'), may hold values from 0 to 255, as said below
- sign_vector: int32 [32, 128], P('context'), may hold values from -1 to 1, as said below
- exponents: int32 [8, 32], P('dp', 'context'), may hold values from 0 to 3
Outputs:
- rotated_grad: float32 [32, 128, 1024], P('context', 'dp', 'tensor')
Inputs may be any that keep to these rules, and one draw needn't show every extreme that they name: `doc_stretches`: each row gives the lengths in units of 128 tokens of 10 documents; they sum to 64. The second document is one of the longest, exactly 8 units, and begins 512 - 128 tokens after a multiple of 512 tokens. `stretch_order`: each row is a permutation of the 256 sequence blocks. Sequence blocks d * 16 to d * 16 + 15 belong to index d of context; the 16 stored blocks of one index of context hold at most 1 block belonging to any one index. `sign_vector`: every entry is 1 or -1.
All inputs are finite; a program needn't handle non-finite values.
Results may differ from a plain program's by a relative error of at most 0.0075.
Values may be sent and summed in bfloat16 or wider, within the bound.
No kernel may reach another device: no remote copies, remote signals or barrier semaphores. Data moves between devices by JAX's collectives and lax.ppermute only.
A program may use at most 64 MiB of HBM per device.

v0:
```python
import math
import jax
import jax.numpy as jnp
from jax import lax
from jax.sharding import PartitionSpec as P

HD = 128
GROUP = 4
BLK = 32
PAD = 128
HB = 128


def passed_along(block, axis, distance):
    devices = range(lax.axis_size(axis))
    route = [(i - distance, i) for i in devices if i - distance in devices]
    return lax.ppermute(block, axis, route)


def hadamard_table(table_size):
    index_row = jnp.arange(table_size, dtype=jnp.int32)
    common = jnp.bitwise_and(index_row[:, None], index_row[None, :])
    parity = jnp.zeros((table_size, table_size), jnp.int32)
    for bit_pos in range(table_size.bit_length() - 1):
        parity = parity + jnp.bitwise_and(jnp.right_shift(common, bit_pos), 1)
    signed = 1 - 2 * jnp.bitwise_and(parity, 1)
    return signed.astype(jnp.float32) * float(table_size) ** (-0.5)


def doc_of(position, ends_row):
    return jnp.sum(((position // PAD)[:, None] >= ends_row[None, :]).astype(jnp.int32), axis=1)


def live_pairs(query_pos, query_doc, key_pos, key_doc):
    return (query_doc[:, None] == key_doc[None, :]) & (key_pos[None, :] <= query_pos[:, None])


def block_grads(query_blk, grad_blk, lse_blk, dots_blk, key_blk, value_blk, live):
    scale = HD ** (-0.5)
    scores = (
        jnp.einsum("ghqd,gkd->ghqk", query_blk, key_blk, preferred_element_type=jnp.float32) * scale
    )
    probs = jnp.where(
        live[None, None], jnp.exp(scores - lse_blk.astype(jnp.float32)[..., None]), 0.0
    )
    value_part = jnp.einsum(
        "ghqk,ghqd->gkd", probs.astype(jnp.bfloat16), grad_blk, preferred_element_type=jnp.float32
    )
    dprobs = jnp.einsum("ghqd,gkd->ghqk", grad_blk, value_blk, preferred_element_type=jnp.float32)
    dscores = (probs * (dprobs - dots_blk.astype(jnp.float32)[..., None])).astype(jnp.bfloat16)
    key_part = (
        jnp.einsum("ghqk,ghqd->gkd", dscores, query_blk, preferred_element_type=jnp.float32) * scale
    )
    return (key_part, value_part)


def per_device(
    layer_input,
    queries,
    key_states,
    value_states,
    out_grad,
    log_sums,
    grad_dots,
    doc_stretches,
    stretch_order,
    sign_vector,
    exponents,
):
    local_tokens = queries.shape[2]
    local_kv = key_states.shape[1]
    local_cols = 2 * local_kv * HD
    order_row = stretch_order[0]
    ends_row = jnp.cumsum(doc_stretches[0])
    groups = lax.axis_size("context")
    slot_count = local_tokens // BLK
    capacity = max(1, slot_count // groups)
    device_id = lax.axis_index("context")
    order_grid = order_row.reshape(groups, slot_count)
    own_order = lax.dynamic_slice_in_dim(order_row, device_id * slot_count, slot_count, 0)
    own_target = own_order // slot_count
    slot_ids = jnp.arange(slot_count, dtype=jnp.int32)
    earlier = slot_ids[None, :] < slot_ids[:, None]
    send_rank = jnp.sum(
        jnp.where(earlier & (own_target[None, :] == own_target[:, None]), 1, 0), axis=1
    )
    send_row = own_target * capacity + send_rank
    buffer_ids = jnp.arange(groups * capacity, dtype=jnp.int32)
    send_table = (buffer_ids[:, None] == send_row[None, :]).astype(jnp.bfloat16)
    wanted = device_id * slot_count + slot_ids
    stretch_ids = jnp.arange(order_row.shape[0], dtype=jnp.int32)
    stored_at = jnp.sum(
        jnp.where(order_row[None, :] == wanted[:, None], stretch_ids[None, :], 0), axis=1
    )
    source = stored_at // slot_count
    source_slot = stored_at % slot_count
    source_orders = jnp.take(order_grid, source, axis=0)
    same_target = source_orders // slot_count == device_id
    recv_rank = jnp.sum(
        jnp.where(same_target & (slot_ids[None, :] < source_slot[:, None]), 1, 0), axis=1
    )
    recv_row = source * capacity + recv_rank
    recv_table = (recv_row[:, None] == buffer_ids[None, :]).astype(jnp.bfloat16)

    def pack(array):
        blocks = array[0].reshape(array.shape[1], slot_count, -1)
        return jnp.einsum(
            "rt,htx->rhx", send_table, blocks, preferred_element_type=jnp.float32
        ).astype(jnp.bfloat16)

    def unpack(packed):
        placed = jnp.einsum(
            "sr,rhx->hsx", recv_table, packed, preferred_element_type=jnp.float32
        ).astype(jnp.bfloat16)
        return placed.reshape(packed.shape[1], local_tokens, -1)

    moved = (
        lax.all_to_all(pack(queries), "context", split_axis=0, concat_axis=0, tiled=True),
        lax.all_to_all(pack(out_grad), "context", split_axis=0, concat_axis=0, tiled=True),
        lax.all_to_all(pack(key_states), "context", split_axis=0, concat_axis=0, tiled=True),
        lax.all_to_all(pack(value_states), "context", split_axis=0, concat_axis=0, tiled=True),
        lax.all_to_all(pack(log_sums), "context", split_axis=0, concat_axis=0, tiled=True),
        lax.all_to_all(pack(grad_dots), "context", split_axis=0, concat_axis=0, tiled=True),
    )
    query_sorted = unpack(moved[0])
    grad_sorted = unpack(moved[1])
    key_sorted = unpack(moved[2])
    value_sorted = unpack(moved[3])
    lse_sorted = unpack(moved[4])[:, :, 0]
    dots_sorted = unpack(moved[5])[:, :, 0]
    total_len = local_tokens * groups
    longest_tokens = max(total_len // PAD // 8, local_tokens // PAD) * PAD
    reach = (local_tokens - PAD + longest_tokens - 1) // local_tokens
    query_list = [query_sorted]
    grad_list = [grad_sorted]
    lse_list = [lse_sorted]
    dots_list = [dots_sorted]
    for ahead in range(1, reach + 1):
        later = passed_along(
            (query_sorted, grad_sorted, lse_sorted, dots_sorted), "context", -ahead
        )
        query_list.append(later[0])
        grad_list.append(later[1])
        lse_list.append(later[2])
        dots_list.append(later[3])
    all_query = jnp.concatenate(query_list, axis=1)
    all_grad = jnp.concatenate(grad_list, axis=1)
    all_lse = jnp.concatenate(lse_list, axis=1)
    all_dots = jnp.concatenate(dots_list, axis=1)
    total_rows = all_query.shape[1]
    query_pos_all = device_id * local_tokens + jnp.arange(total_rows, dtype=jnp.int32)
    query_doc_all = doc_of(query_pos_all, ends_row)
    key_pos_own = device_id * local_tokens + jnp.arange(local_tokens, dtype=jnp.int32)
    key_doc_own = doc_of(key_pos_own, ends_row)
    step_len = math.gcd(total_rows, 640)

    def ahead_block(index_val, running):
        offset = index_val * step_len
        query_blk = lax.dynamic_slice_in_dim(all_query, offset, step_len, 1).reshape(
            local_kv, GROUP, step_len, HD
        )
        grad_blk = lax.dynamic_slice_in_dim(all_grad, offset, step_len, 1).reshape(
            local_kv, GROUP, step_len, HD
        )
        lse_blk = lax.dynamic_slice_in_dim(all_lse, offset, step_len, 1).reshape(
            local_kv, GROUP, step_len
        )
        dots_blk = lax.dynamic_slice_in_dim(all_dots, offset, step_len, 1).reshape(
            local_kv, GROUP, step_len
        )
        query_pos = lax.dynamic_slice_in_dim(query_pos_all, offset, step_len, 0)
        query_doc = lax.dynamic_slice_in_dim(query_doc_all, offset, step_len, 0)
        live = live_pairs(query_pos, query_doc, key_pos_own, key_doc_own)
        key_part, value_part = block_grads(
            query_blk, grad_blk, lse_blk, dots_blk, key_sorted, value_sorted, live
        )
        return (running[0] + key_part, running[1] + value_part)

    empty = jnp.zeros((local_kv, local_tokens, HD), jnp.float32)
    key_total, value_total = lax.fori_loop(0, total_rows // step_len, ahead_block, (empty, empty))
    stacked = jnp.stack([key_total, value_total], axis=1)
    sorted_rows = (
        jnp.transpose(stacked, (2, 0, 1, 3))
        .reshape(slot_count, BLK * local_cols)
        .astype(jnp.bfloat16)
    )
    outgoing = jnp.einsum(
        "sr,sx->rx", recv_table, sorted_rows, preferred_element_type=jnp.float32
    ).astype(jnp.bfloat16)
    returned = lax.all_to_all(outgoing, "context", split_axis=0, concat_axis=0, tiled=True)
    stored_rows = jnp.einsum(
        "rt,rx->tx", send_table, returned, preferred_element_type=jnp.float32
    ).astype(jnp.bfloat16)
    kv_local = stored_rows.reshape(local_tokens, local_cols)[None]
    full_input = lax.all_gather(layer_input, "tensor", axis=2, tiled=True)
    row_input = lax.all_to_all(full_input, "context", split_axis=2, concat_axis=1, tiled=True)
    span = row_input[0]
    member_grad = jnp.einsum(
        "td,tc->dc",
        span,
        lax.all_gather(kv_local, "context", axis=1, tiled=True)[0],
        preferred_element_type=jnp.float32,
    )
    local_blocks = sign_vector.shape[0]
    had = hadamard_table(HB)
    shaped = (
        member_grad.reshape(local_blocks, HB, local_cols)
        * sign_vector.astype(jnp.float32)[:, :, None]
    )
    rotated = jnp.einsum("ij,bjc->bic", had, shaped, precision=lax.Precision.HIGHEST)
    factor = 1.0 / jnp.left_shift(jnp.int32(1), exponents[0]).astype(jnp.float32)
    quantized = (rotated * factor[:, None, None]).astype(jnp.bfloat16)
    spread = lax.all_to_all(quantized[None], "dp", split_axis=2, concat_axis=0, tiled=True)
    return jnp.sum(spread.astype(jnp.float32), axis=0)


def solution(mesh):
    return jax.shard_map(
        per_device,
        mesh=mesh,
        in_specs=(
            P("dp", "context", "tensor"),
            P("dp", "tensor", "context", None),
            P("dp", "tensor", "context", None),
            P("dp", "tensor", "context", None),
            P("dp", "tensor", "context", None),
            P("dp", "tensor", "context"),
            P("dp", "tensor", "context"),
            P("dp", None),
            P("dp", None),
            P("context", None),
            P("dp", "context"),
        ),
        out_specs=P("context", "dp", "tensor"),
        check_vma=False,
    )
```

profile of v0, /device:TPU:6, one launch (start us, length us, event | category | flops | bytes accessed | tf_op | source)
XLA Modules:
  0.0 429.9 jit_solution(6349806971333252527)
XLA Ops:
  12.0 7.2 %all-to-all-start.2 = ((bf16[16,4,32]{2,1,0:T(4,128)(2,1)}), bf16[16,4,32]{2,1,0:T(4,128)(2,1)S(1)}, u32[]{:S(2)}, u32[]{:S(2)}) async-start(bf16[16,4,32]{2,1,0:T(4,128)(2,1)} %copy.89), calls=%async_computation.2 | async-start | bytes 32768 | tf_op jit(solution)/shard_map/all_to_all | solution.py:122
  22.9 4.0 all-to-all-done.2
  26.9 3.5 all-to-all-start.5
  38.2 7.1 %all-to-all-start = ((bf16[16,4,4096]{2,1,0:T(4,128)(2,1)}), bf16[16,4,4096]{2,1,0:T(4,128)(2,1)S(1)}, u32[]{:S(2)}, u32[]{:S(2)}) async-start(bf16[16,4,4096]{2,1,0:T(4,128)(2,1)} %copy.86), calls=%async_computation | async-start | bytes 1048576 | tf_op jit(solution)/shard_map/all_to_all | solution.py:118
  45.8 15.6 %all-to-all-done = bf16[16,4,4096]{2,1,0:T(4,128)(2,1)S(1)} async-done(((bf16[16,4,4096]{2,1,0:T(4,128)(2,1)}), bf16[16,4,4096]{2,1,0:T(4,128)(2,1)S(1)}, u32[]{:S(2)}, u32[]{:S(2)}) %all-to-all-start) | async-done | bytes 524320 | tf_op jit(solution)/shard_map/all_to_all | solution.py:118
  61.3 4.2 all-to-all-start.3
  71.3 8.8 %collective-permute-done.3 = bf16[4,512]{1,0:T(4,128)(2,1)S(1)} collective-permute-done((bf16[4,512]{1,0:T(4,128)(2,1)S(1)}, bf16[4,512]{1,0:T(4,128)(2,1)S(1)}, u32[]{:S(2)}, u32[]{:S(2)}) %collective-permute-start.3) | collective-permute-done | bytes 4128 | tf_op jit(solution)/shard_map/ppermute | solution.py:17
  83.4 9.8 %all-to-all-start.1 = ((bf16[16,2,2048]{2,1,0:T(2,128)(2,1)}), bf16[16,2,2048]{2,1,0:T(2,128)(2,1)S(1)}, u32[]{:S(2)}, u32[]{:S(2)}) async-start(bf16[16,2,2048]{2,1,0:T(2,128)(2,1)} %reshape.396), calls=%async_computation.1 | async-start | bytes 262144 | tf_op jit(solution)/shard_map/all_to_all | solution.py:120
  95.2 16.5 %all-to-all-done.1 = bf16[16,2,2048]{2,1,0:T(2,128)(2,1)S(1)} async-done(((bf16[16,2,2048]{2,1,0:T(2,128)(2,1)}), bf16[16,2,2048]{2,1,0:T(2,128)(2,1)S(1)}, u32[]{:S(2)}, u32[]{:S(2)}) %all-to-all-start.1) | async-done | bytes 131104 | tf_op jit(solution)/shard_map/all_to_all | solution.py:120
  111.8 5.7 %all-to-all-start.4 = ((bf16[16,2,2048]{2,1,0:T(2,128)(2,1)}), bf16[16,2,2048]{2,1,0:T(2,128)(2,1)S(1)}, u32[]{:S(2)}, u32[]{:S(2)}) async-start(bf16[16,2,2048]{2,1,0:T(2,128)(2,1)} %reshape.398), calls=%async_computation.4 | async-start | bytes 262144 | tf_op jit(solution)/shard_map/all_to_all | solution.py:121
  119.3 6.9 %all-to-all-done.4 = bf16[16,2,2048]{2,1,0:T(2,128)(2,1)S(1)} async-done(((bf16[16,2,2048]{2,1,0:T(2,128)(2,1)}), bf16[16,2,2048]{2,1,0:T(2,128)(2,1)S(1)}, u32[]{:S(2)}, u32[]{:S(2)}) %all-to-all-start.4) | async-done | bytes 131104 | tf_op jit(solution)/shard_map/all_to_all | solution.py:121
  126.7 2.3 pad_maximum_fusion
  129.0 1.3 pad_maximum_fusion.1
  130.3 44.5 %while.16 = (s32[]{:T(128)}, f32[1,512,128]{2,1,0:T(8,128)S(1)}, f32[1,512,128]{2,1,0:T(8,128)S(1)}, s32[1536]{0:T(1024)S(1)}, s32[512]{0:T(512)S(1)}, /*index=5...) while((s32[]{:T(128)}, f32[1,512,128]{2,1,0:T(8,128)S(1)}, ...), condition=%wide.region_7.8_spmd.clone, body=%wide.region_6.7_spmd.clone.sunk | while | flops 270796288 | bytes 5133045 | solution.py:180
  130.7 1.3 fusion.160
  132.0 1.7 fusion.161
  134.4 1.3 fusion.160
  135.7 1.7 fusion.161
  138.1 1.3 fusion.160
  139.4 1.7 fusion.161
  141.8 1.3 fusion.160
  143.1 1.7 fusion.161
  145.5 1.3 fusion.160
  146.8 1.7 fusion.161
  149.2 1.3 fusion.160
  150.5 1.7 fusion.161
  152.9 1.3 fusion.160
  154.2 1.7 fusion.161
  156.6 1.3 fusion.160
  157.9 1.7 fusion.161
  160.3 1.3 fusion.160
  161.7 1.7 fusion.161
  165.4 1.7 fusion.161
  167.8 1.3 fusion.160
  169.1 1.7 fusion.161
  171.5 1.3 fusion.160
  172.8 1.7 fusion.161
  176.7 17.0 %all_to_all.66 = bf16[16,2,4096]{2,1,0:T(2,128)(2,1)S(1)} all-to-all(bf16[16,2,4096]{2,1,0:T(2,128)(2,1)S(1)} %reshape.400), channel_id=1, replica_groups=mesh['dp'=8,'context'=16,'tensor'=4] {'context'}, dimensions={0} | all-to-all | bytes 524288 | tf_op jit(solution)/shard_map/all_to_all | solution.py:190
  194.0 18.9 %copy.98 = bf16[1,512,4096]{1,0,2:T(2,128)(2,1)} copy(bf16[1,512,4096]{2,1,0:T(8,128)(2,1)} %all-gather.5.cloned.1.call-done) | data formatting | bytes 8388608 | tf_op jit(solution)/shard_map/all_gather | solution.py:195
  212.9 28.5 %reduce.7 = bf16[4096,512]{1,0:T(8,128)(2,1)} reduce(bf16[4096,1,512]{2,1,0:T(2,128)(2,1)} %bitcast.157, bf16[]{:T(256)} %broadcast.474), dimensions={1}, to_apply=%bitcast.136.reduce_sub_computation | reduce | bytes 8388610
  241.4 11.4 %reshape.394 = bf16[16,2,65536]{2,1,0:T(2,128)(2,1)} reshape(bf16[4096,512]{1,0:T(8,128)(2,1)} %reduce.7) | data formatting | bytes 8388608
  252.8 4.7 %all-to-all-start.7 = ((bf16[16,2,65536]{2,1,0:T(2,128)(2,1)}), bf16[16,2,65536]{2,1,0:T(2,128)(2,1)}, u32[]{:S(2)}, u32[]{:S(2)}) async-start(bf16[16,2,65536]{2,1,0:T(2,128)(2,1)} %reshape.394), calls=%async_computation.7 | async-start | bytes 8388608 | tf_op jit(solution)/shard_map/all_to_all | solution.py:196
  258.9 112.6 %all-to-all-done.7 = bf16[16,2,65536]{2,1,0:T(2,128)(2,1)} async-done(((bf16[16,2,65536]{2,1,0:T(2,128)(2,1)}), bf16[16,2,65536]{2,1,0:T(2,128)(2,1)}, u32[]{:S(2)}, u32[]{:S(2)}) %all-to-all-start.7) | async-done | bytes 4194336 | tf_op jit(solution)/shard_map/all_to_all | solution.py:196
  371.4 12.3 %reshape.395 = bf16[4096,1,512]{2,1,0:T(2,128)(2,1)} reshape(bf16[16,2,65536]{2,1,0:T(2,128)(2,1)} %all-to-all-done.7) | data formatting | bytes 8388608
  383.8 6.5 %copy.108 = bf16[1,512,4096]{1,2,0:T(8,128)(2,1)} copy(bf16[1,512,4096]{1,0,2:T(2,128)(2,1)} %bitcast.158) | data formatting | bytes 8388608
  390.3 6.4 %copy.99 = bf16[1,16,512,256]{3,2,1,0:T(8,128)(2,1)} copy(bf16[1,16,512,256]{2,3,1,0:T(8,128)(2,1)} %bitcast.159) | data formatting | bytes 8388608 | tf_op jit(solution)/shard_map/all_to_all | solution.py:196
  396.7 5.2 %fusion.34 = f32[256,256]{0,1:T(8,128)S(1)} fusion(bf16[8192,256]{1,0:T(8,128)(2,1)} %bitcast.160, bf16[1,8192,256]{2,1,0:T(8,128)(2,1)} %all-gather.3.cloned.1.call-done), kind=kOutput, calls=%fused_computation.48 | convolution fusion | flops 1073741824 | bytes 8650752 | tf_op jit(solution)/shard_map/td,tc->dc/dot_general | solution.py:198
  402.6 19.2 %all_to_all.67 = bf16[1,2,128,256]{3,1,0,2:T(2,128)(2,1)S(1)} all-to-all(bf16[1,2,128,256]{3,1,0,2:T(2,128)(2,1)S(1)} %copy.101), channel_id=1, replica_groups=mesh['dp'=8,'context'=16,'tensor'=4] {'dp'}, dimensions={2} | all-to-all | bytes 262144 | tf_op jit(solution)/shard_map/all_to_all | solution.py:213
  (190 shorter events, 43.7 us)
Async XLA Ops:
  7.4 13.5 %copy-start.3 = (s32[1,256]{1,0:T(1,128)S(1)}, s32[1,256]{1,0:T(1,128)}, u32[]{:S(2)}) copy-start(s32[1,256]{1,0:T(1,128)} %param.21) | copy-start | bytes 3076
  7.4 13.7 %copy-start.1 = (bf16[1,1,512,128]{3,2,1,0:T(8,128)(2,1)S(1)}, bf16[1,1,512,128]{3,2,1,0:T(8,128)(2,1)}, u32[]{:S(2)}) copy-start(bf16[1,1,512,128]{3,2,1,0:T(8,128)(2,1)} %param.15) | copy-start | bytes 393220
  7.4 13.9 %copy-start = (bf16[1,4,512,128]{3,2,1,0:T(8,128)(2,1)S(1)}, bf16[1,4,512,128]{3,2,1,0:T(8,128)(2,1)}, u32[]{:S(2)}) copy-start(bf16[1,4,512,128]{3,2,1,0:T(8,128)(2,1)} %param.17) | copy-start | bytes 1572868
  7.4 14.4 %copy-start.2 = (bf16[1,1,512,128]{3,2,1,0:T(8,128)(2,1)S(1)}, bf16[1,1,512,128]{3,2,1,0:T(8,128)(2,1)}, u32[]{:S(2)}) copy-start(bf16[1,1,512,128]{3,2,1,0:T(8,128)(2,1)} %param.16) | copy-start | bytes 393220
  7.4 14.5 %copy-start.4 = (bf16[1,4,512]{2,1,0:T(4,128)(2,1)S(1)}, bf16[1,4,512]{2,1,0:T(4,128)(2,1)}, u32[]{:S(2)}) copy-start(bf16[1,4,512]{2,1,0:T(4,128)(2,1)} %param.19) | copy-start | bytes 12292
  7.4 23.0 %copy-start.6 = (s32[1,10]{1,0:T(1,128)S(1)}, s32[1,10]{1,0:T(1,128)}, u32[]{:S(2)}) copy-start(s32[1,10]{1,0:T(1,128)} %param.20) | copy-start | bytes 124
  7.4 186.6 %all-gather.5.cloned.1.call-start = ((), (), s32[]{:S(2)}) async-start(), calls=%async_computation.10 | async-start | bytes 5242880 | tf_op jit(solution)/shard_map/all_gather | solution.py:195
  12.0 14.8 %all-to-all-start.2 = ((bf16[16,4,32]{2,1,0:T(4,128)(2,1)}), bf16[16,4,32]{2,1,0:T(4,128)(2,1)S(1)}, u32[]{:S(2)}, u32[]{:S(2)}) async-start(bf16[16,4,32]{2,1,0:T(4,128)(2,1)} %copy.89), calls=%async_computation.2 | async-start | bytes 32768 | tf_op jit(solution)/shard_map/all_to_all | solution.py:122
  26.9 11.3 %all-to-all-start.5 = ((bf16[16,4,32]{2,1,0:T(4,128)(2,1)}), bf16[16,4,32]{2,1,0:T(4,128)(2,1)S(1)}, u32[]{:S(2)}, u32[]{:S(2)}) async-start(bf16[16,4,32]{2,1,0:T(4,128)(2,1)} %copy.94), calls=%async_computation.5 | async-start | bytes 32768 | tf_op jit(solution)/shard_map/all_to_all | solution.py:123
  38.2 23.2 %all-to-all-start = ((bf16[16,4,4096]{2,1,0:T(4,128)(2,1)}), bf16[16,4,4096]{2,1,0:T(4,128)(2,1)S(1)}, u32[]{:S(2)}, u32[]{:S(2)}) async-start(bf16[16,4,4096]{2,1,0:T(4,128)(2,1)} %copy.86), calls=%async_computation | async-start | bytes 1048576 | tf_op jit(solution)/shard_map/all_to_all | solution.py:118
  61.3 22.0 %all-to-all-start.3 = ((bf16[16,4,4096]{2,1,0:T(4,128)(2,1)}), bf16[16,4,4096]{2,1,0:T(4,128)(2,1)S(1)}, u32[]{:S(2)}, u32[]{:S(2)}) async-start(bf16[16,4,4096]{2,1,0:T(4,128)(2,1)} %copy.91), calls=%async_computation.3 | async-start | bytes 1048576 | tf_op jit(solution)/shard_map/all_to_all | solution.py:119
  65.8 14.2 %collective-permute-start.3 = (bf16[4,512]{1,0:T(4,128)(2,1)S(1)}, bf16[4,512]{1,0:T(4,128)(2,1)S(1)}, u32[]{:S(2)}, u32[]{:S(2)}) collective-permute-start(bf16[4,512]{1,0:T(4,128)(2,1)S(1)} %squeeze_reshape.6), channel_id=1, source_target_pairs={{8,0},{12,4},{16,8},{20,12},{24,16},{28,20},{32,24},{36,28},{40,32... | collective-permute-start | bytes 12296 | tf_op jit(solution)/shard_map/ppermute | solution.py:17
  67.1 13.0 %collective-permute-start.2 = (bf16[4,512]{1,0:T(4,128)(2,1)S(1)}, bf16[4,512]{1,0:T(4,128)(2,1)S(1)}, u32[]{:S(2)}, u32[]{:S(2)}) collective-permute-start(bf16[4,512]{1,0:T(4,128)(2,1)S(1)} %squeeze_reshape.6), channel_id=1, source_target_pairs={{4,0},{8,4},{12,8},{16,12},{20,16},{24,20},{28,24},{32,28},{36,32}... | collective-permute-start | bytes 12296 | tf_op jit(solution)/shard_map/ppermute | solution.py:17
  68.7 48.7 %collective-permute-start.7 = (bf16[4,512]{1,0:T(4,128)(2,1)S(1)}, bf16[4,512]{1,0:T(4,128)(2,1)S(1)}, u32[]{:S(2)}, u32[]{:S(2)}) collective-permute-start(bf16[4,512]{1,0:T(4,128)(2,1)S(1)} %squeeze_reshape.7), channel_id=1, source_target_pairs={{8,0},{12,4},{16,8},{20,12},{24,16},{28,20},{32,24},{36,28},{40,32... | collective-permute-start | bytes 12296 | tf_op jit(solution)/shard_map/ppermute | solution.py:17
  70.0 48.8 %collective-permute-start.6 = (bf16[4,512]{1,0:T(4,128)(2,1)S(1)}, bf16[4,512]{1,0:T(4,128)(2,1)S(1)}, u32[]{:S(2)}, u32[]{:S(2)}) collective-permute-start(bf16[4,512]{1,0:T(4,128)(2,1)S(1)} %squeeze_reshape.7), channel_id=1, source_target_pairs={{4,0},{8,4},{12,8},{16,12},{20,16},{24,20},{28,24},{32,28},{36,32}... | collective-permute-start | bytes 12296 | tf_op jit(solution)/shard_map/ppermute | solution.py:17
  80.8 45.9 %collective-permute-start.1 = (bf16[4,512,128]{2,1,0:T(8,128)(2,1)S(1)}, bf16[4,512,128]{2,1,0:T(8,128)(2,1)S(1)}, u32[]{:S(2)}, u32[]{:S(2)}) collective-permute-start(bf16[4,512,128]{2,1,0:T(8,128)(2,1)S(1)} %reshape.358), channel_id=1, source_target_pairs={{8,0},{12,4},{16,8},{20,12},{24,16},{28,20},{32,24},{36,28},{40,32... | collective-permute-start | bytes 1572872 | tf_op jit(solution)/shard_map/ppermute | solution.py:17
  82.1 44.6 %collective-permute-start = (bf16[4,512,128]{2,1,0:T(8,128)(2,1)S(1)}, bf16[4,512,128]{2,1,0:T(8,128)(2,1)}, u32[]{:S(2)}, u32[]{:S(2)}) collective-permute-start(bf16[4,512,128]{2,1,0:T(8,128)(2,1)S(1)} %reshape.358), channel_id=1, source_target_pairs={{4,0},{8,4},{12,8},{16,12},{20,16},{24,20},{28,24},{32,28},{36,32}... | collective-permute-start | bytes 1572872 | tf_op jit(solution)/shard_map/ppermute | solution.py:17
  83.4 28.4 %all-to-all-start.1 = ((bf16[16,2,2048]{2,1,0:T(2,128)(2,1)}), bf16[16,2,2048]{2,1,0:T(2,128)(2,1)S(1)}, u32[]{:S(2)}, u32[]{:S(2)}) async-start(bf16[16,2,2048]{2,1,0:T(2,128)(2,1)} %reshape.396), calls=%async_computation.1 | async-start | bytes 262144 | tf_op jit(solution)/shard_map/all_to_all | solution.py:120
  93.9 35.1 %collective-permute-start.5 = (bf16[4,512,128]{2,1,0:T(8,128)(2,1)S(1)}, bf16[4,512,128]{2,1,0:T(8,128)(2,1)}, u32[]{:S(2)}, u32[]{:S(2)}) collective-permute-start(bf16[4,512,128]{2,1,0:T(8,128)(2,1)S(1)} %reshape.362), channel_id=1, source_target_pairs={{8,0},{12,4},{16,8},{20,12},{24,16},{28,20},{32,24},{36,28},{40,32... | collective-permute-start | bytes 1572872 | tf_op jit(solution)/shard_map/ppermute | solution.py:17
  111.8 14.4 %all-to-all-start.4 = ((bf16[16,2,2048]{2,1,0:T(2,128)(2,1)}), bf16[16,2,2048]{2,1,0:T(2,128)(2,1)S(1)}, u32[]{:S(2)}, u32[]{:S(2)}) async-start(bf16[16,2,2048]{2,1,0:T(2,128)(2,1)} %reshape.398), calls=%async_computation.4 | async-start | bytes 262144 | tf_op jit(solution)/shard_map/all_to_all | solution.py:121
  117.5 11.6 %collective-permute-start.4 = (bf16[4,512,128]{2,1,0:T(8,128)(2,1)S(1)}, bf16[4,512,128]{2,1,0:T(8,128)(2,1)}, u32[]{:S(2)}, u32[]{:S(2)}) collective-permute-start(bf16[4,512,128]{2,1,0:T(8,128)(2,1)S(1)} %reshape.362), channel_id=1, source_target_pairs={{4,0},{8,4},{12,8},{16,12},{20,16},{24,20},{28,24},{32,28},{36,32}... | collective-permute-start | bytes 1572872 | tf_op jit(solution)/shard_map/ppermute | solution.py:17
  252.8 6.0 %copy-start.5 = (s32[2,128]{1,0:T(2,128)S(1)}, s32[2,128]{1,0:T(2,128)}, u32[]{:S(2)}) copy-start(s32[2,128]{1,0:T(2,128)} %param.22) | copy-start | bytes 3076
  252.8 6.0 %copy-start.7 = (s32[1,2]{1,0:T(1,128)S(1)}, s32[1,2]{1,0:T(1,128)}, u32[]{:S(2)}) copy-start(s32[1,2]{1,0:T(1,128)} %param.23) | copy-start | bytes 28
  252.8 118.6 %all-to-all-start.7 = ((bf16[16,2,65536]{2,1,0:T(2,128)(2,1)}), bf16[16,2,65536]{2,1,0:T(2,128)(2,1)}, u32[]{:S(2)}, u32[]{:S(2)}) async-start(bf16[16,2,65536]{2,1,0:T(2,128)(2,1)} %reshape.394), calls=%async_computation.7 | async-start | bytes 8388608 | tf_op jit(solution)/shard_map/all_to_all | solution.py:196
  257.5 139.2 %all-gather.3.cloned.1.call-start = ((), (), s32[]{:S(2)}) async-start(), calls=%async_computation.9 | async-start | bytes 4456448 | tf_op jit(solution)/shard_map/all_gather | solution.py:201
Sparse Core Ops, SparseCore 0:
  10.3 56.3 all-gather.4
Sparse Core Ops, SparseCore 1:
  260.1 110.8 all-gather.2
where the time goes:
time: 433 us; the launch traced here: 430 us
  waiting for transfers between devices  165 us (38%)
  local copies, waits for them, and re-layouts  69.7 us (16%)
  starting transfers between devices  52.6 us (12%)
  matrix products  49.4 us (11%)
  other arithmetic  40.5 us (9%)
  blocking collectives  36.2 us (8%)
  between operations  15.5 us (4%)
    all_to_all x1, waiting for transfers between devices, per_device(): lax.all_to_all(full_input, 'context', split_axis=2, concat_axis=1, tiled=...  113 us
    unnamed x27, local copies, waits for them, and re-layouts  33.5 us
    unnamed x4, other arithmetic  29.1 us
    dot_general x12, matrix products, block_grads(): jnp.einsum('ghqk,ghqd->gkd', dscores, query_blk, preferred_element_type=j...  19.9 us
    all_to_all x1, blocking collectives, per_device(): lax.all_to_all(quantized[None], 'dp', split_axis=2, concat_axis=0, tiled=...  19.2 us
    all_gather x1, local copies, waits for them, and re-layouts, per_device(): full_input = lax.all_gather(layer_input, 'tensor', axis=2, tiled=True)  18.9 us
    all_to_all x1, blocking collectives, per_device(): lax.all_to_all(outgoing, 'context', split_axis=0, concat_axis=0, tiled=True)  17 us
    all_to_all x1, waiting for transfers between devices, per_device(): lax.all_to_all(pack(key_states), 'context', split_axis=0, concat_axis=0,...  16.5 us
  transfers between devices with their start and end apart: 17, of which 6 were waited for; matrix products, arithmetic and copies ran while one was open for 22% of the time, Pallas kernels for 0%

commit v1 on v0

--- a/solution.py
+++ b/solution.py
@@ -192,7 +192,10 @@
         "rt,rx->tx", send_table, returned, preferred_element_type=jnp.float32
     ).astype(jnp.bfloat16)
     kv_local = stored_rows.reshape(local_tokens, local_cols)[None]
-    full_input = lax.all_gather(layer_input, "tensor", axis=2, tiled=True)
+    peers = lax.axis_size("tensor")
+    shards = jnp.stack([layer_input for _ in range(peers)])
+    shards = lax.all_to_all(shards, "tensor", split_axis=0, concat_axis=0)
+    full_input = jnp.concatenate(shards, axis=2)
     row_input = lax.all_to_all(full_input, "context", split_axis=2, concat_axis=1, tiled=True)
     span = row_input[0]
     member_grad = jnp.einsum(

time: 433 us -> 480 us (1.11)
  waiting for transfers between devices: 165 us -> 220 us
  blocking collectives: 36.2 us -> 17.6 us
  starting transfers between devices: 52.6 us -> 67.9 us
    all_to_all x0 -> x2, waiting for transfers between devices: none -> 58.6 us  [the longest x1 47.9 us: per_device(): shards = lax.all_to_all(shards, 'tensor', split_axis=0, concat_axis=0)]
    all_gather x1 -> x0, local copies, waits for them, and re-layouts: 18.9 us -> none  [per_device(): full_input = lax.all_gather(layer_input, 'tensor', axis=2, tiled=True)]
    all_to_all x1 -> x0, blocking collectives: 17 us -> none  [per_device(): lax.all_to_all(outgoing, 'context', split_axis=0, concat_axis=0, tiled=True)]
    all_to_all x0 -> x2, starting transfers between devices: none -> 13 us  [the longest x1 6.94 us: per_device(): shards = lax.all_to_all(shards, 'tensor', split_axis=0, concat_axis=0)]
    reshape x0 -> x1, local copies, waits for them, and re-layouts: none -> 8.63 us  [per_device(): full_input = jnp.concatenate(shards, axis=2)]
    unnamed x27 -> x25, local copies, waits for them, and re-layouts: 33.5 us -> 34.2 us
  transfers between devices with their start and end apart: 17 -> 18, of which waited for: 6 -> 8; matrix products, arithmetic and copies ran while one was open for 22% -> 10% of each run, Pallas kernels for 0% -> 0%
where the time goes in v1:
time: 480 us; the launch traced here: 476 us
  waiting for transfers between devices  220 us (46%)
  starting transfers between devices  67.9 us (14%)
  local copies, waits for them, and re-layouts  64.9 us (14%)
  matrix products  49.4 us (10%)
  other arithmetic  41.2 us (9%)
  blocking collectives  17.6 us (4%)
  between operations  14 us (3%)
    all_to_all x1, waiting for transfers between devices, per_device(): lax.all_to_all(full_input, 'context', split_axis=2, concat_axis=1, tiled=...  113 us
    all_to_all x1, waiting for transfers between devices, per_device(): shards = lax.all_to_all(shards, 'tensor', split_axis=0, concat_axis=0)  47.9 us
    unnamed x25, local copies, waits for them, and re-layouts  34.2 us
    unnamed x4, other arithmetic  29.1 us
    dot_general x12, matrix products, block_grads(): jnp.einsum('ghqk,ghqd->gkd', dscores, query_blk, preferred_element_type=j...  19.9 us
    all_to_all x1, blocking collectives, per_device(): lax.all_to_all(quantized[None], 'dp', split_axis=2, concat_axis=0, tiled=...  17.6 us
    all_to_all x1, waiting for transfers between devices, per_device(): lax.all_to_all(pack(key_states), 'context', split_axis=0, concat_axis=0,...  16.6 us
    dot_general x12, matrix products, block_grads(): jnp.einsum('ghqd,gkd->ghqk', query_blk, key_blk, preferred_element_type=j...  15.7 us
  transfers between devices with their start and end apart: 18, of which 8 were waited for; matrix products, arithmetic and copies ran while one was open for 10% of the time, Pallas kernels for 0%

profile of v1, /device:TPU:6, one launch (start us, length us, event | category | flops | bytes accessed | tf_op | source)
XLA Modules:
  0.0 476.3 jit_solution(6131176147378753890)
XLA Ops:
  10.5 7.2 %all-to-all-start.2 = ((bf16[16,4,32]{2,1,0:T(4,128)(2,1)}), bf16[16,4,32]{2,1,0:T(4,128)(2,1)S(1)}, u32[]{:S(2)}, u32[]{:S(2)}) async-start(bf16[16,4,32]{2,1,0:T(4,128)(2,1)} %copy.68), calls=%async_computation.2 | async-start | bytes 32768 | tf_op jit(solution)/shard_map/all_to_all | solution.py:122
  23.9 1.4 all-to-all-done.2
  25.3 5.8 %all-to-all-start.5 = ((bf16[16,4,32]{2,1,0:T(4,128)(2,1)}), bf16[16,4,32]{2,1,0:T(4,128)(2,1)S(1)}, u32[]{:S(2)}, u32[]{:S(2)}) async-start(bf16[16,4,32]{2,1,0:T(4,128)(2,1)} %copy.73), calls=%async_computation.5 | async-start | bytes 32768 | tf_op jit(solution)/shard_map/all_to_all | solution.py:123
  38.9 7.2 %all-to-all-start = ((bf16[16,4,4096]{2,1,0:T(4,128)(2,1)}), bf16[16,4,4096]{2,1,0:T(4,128)(2,1)S(1)}, u32[]{:S(2)}, u32[]{:S(2)}) async-start(bf16[16,4,4096]{2,1,0:T(4,128)(2,1)} %copy.65), calls=%async_computation | async-start | bytes 1048576 | tf_op jit(solution)/shard_map/all_to_all | solution.py:118
  46.6 15.6 %all-to-all-done = bf16[16,4,4096]{2,1,0:T(4,128)(2,1)S(1)} async-done(((bf16[16,4,4096]{2,1,0:T(4,128)(2,1)}), bf16[16,4,4096]{2,1,0:T(4,128)(2,1)S(1)}, u32[]{:S(2)}, u32[]{:S(2)}) %all-to-all-start) | async-done | bytes 524320 | tf_op jit(solution)/shard_map/all_to_all | solution.py:118
  62.2 4.2 all-to-all-start.3
  72.1 8.8 %collective-permute-done.3 = bf16[4,512]{1,0:T(4,128)(2,1)S(1)} collective-permute-done((bf16[4,512]{1,0:T(4,128)(2,1)S(1)}, bf16[4,512]{1,0:T(4,128)(2,1)S(1)}, u32[]{:S(2)}, u32[]{:S(2)}) %collective-permute-start.3) | collective-permute-done | bytes 4128 | tf_op jit(solution)/shard_map/ppermute | solution.py:17
  84.2 9.8 %all-to-all-start.1 = ((bf16[16,2,2048]{2,1,0:T(2,128)(2,1)}), bf16[16,2,2048]{2,1,0:T(2,128)(2,1)S(1)}, u32[]{:S(2)}, u32[]{:S(2)}) async-start(bf16[16,2,2048]{2,1,0:T(2,128)(2,1)} %reshape.407), calls=%async_computation.1 | async-start | bytes 262144 | tf_op jit(solution)/shard_map/all_to_all | solution.py:120
  96.1 16.6 %all-to-all-done.1 = bf16[16,2,2048]{2,1,0:T(2,128)(2,1)S(1)} async-done(((bf16[16,2,2048]{2,1,0:T(2,128)(2,1)}), bf16[16,2,2048]{2,1,0:T(2,128)(2,1)S(1)}, u32[]{:S(2)}, u32[]{:S(2)}) %all-to-all-start.1) | async-done | bytes 131104 | tf_op jit(solution)/shard_map/all_to_all | solution.py:120
  112.6 5.7 %all-to-all-start.4 = ((bf16[16,2,2048]{2,1,0:T(2,128)(2,1)}), bf16[16,2,2048]{2,1,0:T(2,128)(2,1)S(1)}, u32[]{:S(2)}, u32[]{:S(2)}) async-start(bf16[16,2,2048]{2,1,0:T(2,128)(2,1)} %reshape.409), calls=%async_computation.4 | async-start | bytes 262144 | tf_op jit(solution)/shard_map/all_to_all | solution.py:121
  120.1 6.9 %all-to-all-done.4 = bf16[16,2,2048]{2,1,0:T(2,128)(2,1)S(1)} async-done(((bf16[16,2,2048]{2,1,0:T(2,128)(2,1)}), bf16[16,2,2048]{2,1,0:T(2,128)(2,1)S(1)}, u32[]{:S(2)}, u32[]{:S(2)}) %all-to-all-start.4) | async-done | bytes 131104 | tf_op jit(solution)/shard_map/all_to_all | solution.py:121
  127.5 2.3 pad_maximum_fusion
  129.9 1.3 pad_maximum_fusion.1
  131.2 44.5 %while.16 = (s32[]{:T(128)}, f32[1,512,128]{2,1,0:T(8,128)S(1)}, f32[1,512,128]{2,1,0:T(8,128)S(1)}, s32[1536]{0:T(1024)S(1)}, s32[512]{0:T(512)S(1)}, /*index=5...) while((s32[]{:T(128)}, f32[1,512,128]{2,1,0:T(8,128)S(1)}, ...), condition=%wide.region_7.8_spmd.clone, body=%wide.region_6.7_spmd.clone.sunk | while | flops 270796288 | bytes 5133045 | solution.py:180
  131.5 1.3 fusion.160
  132.8 1.7 fusion.161
  135.2 1.3 fusion.160
  136.5 1.7 fusion.161
  138.9 1.3 fusion.160
  140.2 1.7 fusion.161
  142.6 1.3 fusion.160
  144.0 1.7 fusion.161
  147.7 1.7 fusion.161
  150.1 1.3 fusion.160
  151.4 1.7 fusion.161
  155.1 1.7 fusion.161
  157.5 1.3 fusion.160
  158.8 1.7 fusion.161
  162.5 1.7 fusion.161
  164.9 1.3 fusion.160
  166.2 1.7 fusion.161
  169.9 1.7 fusion.161
  173.6 1.7 fusion.161
  178.3 6.0 %all-to-all-start.6 = ((bf16[16,2,4096]{2,1,0:T(2,128)(2,1)}), bf16[16,2,4096]{2,1,0:T(2,128)(2,1)S(1)}, u32[]{:S(2)}, u32[]{:S(2)}) async-start(bf16[16,2,4096]{2,1,0:T(2,128)(2,1)} %reshape.411), calls=%async_computation.6 | async-start | bytes 524288 | tf_op jit(solution)/shard_map/all_to_all | solution.py:190
  184.9 10.6 %all-to-all-done.6 = bf16[16,2,4096]{2,1,0:T(2,128)(2,1)S(1)} async-done(((bf16[16,2,4096]{2,1,0:T(2,128)(2,1)}), bf16[16,2,4096]{2,1,0:T(2,128)(2,1)S(1)}, u32[]{:S(2)}, u32[]{:S(2)}) %all-to-all-start.6) | async-done | bytes 262176 | tf_op jit(solution)/shard_map/all_to_all | solution.py:190
  195.5 2.3 stack.22
  197.8 6.9 %all-to-all-start.7 = ((bf16[4,1,512,1024]{2,3,1,0:T(8,128)(2,1)}), bf16[4,1,512,1024]{2,3,1,0:T(8,128)(2,1)}, u32[]{:S(2)}, u32[]{:S(2)}) async-start(bf16[4,1,512,1024]{2,3,1,0:T(8,128)(2,1)} %stack.22), calls=%async_computation.7 | async-start | bytes 8388608 | tf_op jit(solution)/shard_map/all_to_all | solution.py:197
  205.0 47.9 %all-to-all-done.7 = bf16[4,1,512,1024]{2,3,1,0:T(8,128)(2,1)} async-done(((bf16[4,1,512,1024]{2,3,1,0:T(8,128)(2,1)}), bf16[4,1,512,1024]{2,3,1,0:T(8,128)(2,1)}, u32[]{:S(2)}, u32[]{:S(2)}) %all-to-all-start.7) | async-done | bytes 4194336 | tf_op jit(solution)/shard_map/all_to_all | solution.py:197
  252.9 8.6 %copy.111 = bf16[1,512,4096]{1,0,2:T(2,128)(2,1)} copy(bf16[1,512,4096]{1,2,0:T(8,128)(2,1)} %bitcast.29) | data formatting | bytes 8388608 | tf_op jit(solution)/shard_map/reshape | solution.py:198
  261.5 28.5 %reduce.7 = bf16[4096,512]{1,0:T(8,128)(2,1)} reduce(bf16[4096,1,512]{2,1,0:T(2,128)(2,1)} %bitcast.165, bf16[]{:T(256)} %broadcast.477), dimensions={1}, to_apply=%bitcast.154.reduce_sub_computation | reduce | bytes 8388610
  290.0 11.4 %reshape.405 = bf16[16,2,65536]{2,1,0:T(2,128)(2,1)} reshape(bf16[4096,512]{1,0:T(8,128)(2,1)} %reduce.7) | data formatting | bytes 8388608
  301.4 4.7 all-to-all-start.8
  307.5 112.5 %all-to-all-done.8 = bf16[16,2,65536]{2,1,0:T(2,128)(2,1)} async-done(((bf16[16,2,65536]{2,1,0:T(2,128)(2,1)}), bf16[16,2,65536]{2,1,0:T(2,128)(2,1)}, u32[]{:S(2)}, u32[]{:S(2)}) %all-to-all-start.8) | async-done | bytes 4194336 | tf_op jit(solution)/shard_map/all_to_all | solution.py:199
  420.0 12.3 %reshape.406 = bf16[4096,1,512]{2,1,0:T(2,128)(2,1)} reshape(bf16[16,2,65536]{2,1,0:T(2,128)(2,1)} %all-to-all-done.8) | data formatting | bytes 8388608
  432.3 6.5 %copy.89 = bf16[1,512,4096]{1,2,0:T(8,128)(2,1)} copy(bf16[1,512,4096]{1,0,2:T(2,128)(2,1)} %bitcast.166) | data formatting | bytes 8388608
  438.9 6.4 %copy.80 = bf16[1,16,512,256]{3,2,1,0:T(8,128)(2,1)} copy(bf16[1,16,512,256]{2,3,1,0:T(8,128)(2,1)} %bitcast.167) | data formatting | bytes 8388608 | tf_op jit(solution)/shard_map/all_to_all | solution.py:199
  445.3 5.2 %fusion.34 = f32[256,256]{0,1:T(8,128)S(1)} fusion(bf16[8192,256]{1,0:T(8,128)(2,1)} %bitcast.168, bf16[1,8192,256]{2,1,0:T(8,128)(2,1)} %all-gather.2.cloned.1.call-done), kind=kOutput, calls=%fused_computation.48 | convolution fusion | flops 1073741824 | bytes 8650752 | tf_op jit(solution)/shard_map/td,tc->dc/dot_general | solution.py:201
  451.2 17.6 %all_to_all.71 = bf16[1,2,128,256]{3,1,0,2:T(2,128)(2,1)S(1)} all-to-all(bf16[1,2,128,256]{3,1,0,2:T(2,128)(2,1)S(1)} %copy.82), channel_id=1, replica_groups=mesh['dp'=8,'context'=16,'tensor'=4] {'dp'}, dimensions={2} | all-to-all | bytes 262144 | tf_op jit(solution)/shard_map/all_to_all | solution.py:216
  (190 shorter events, 52.1 us)
Async XLA Ops:
  6.5 16.3 %copy-start.1 = (bf16[1,1,512,128]{3,2,1,0:T(8,128)(2,1)S(1)}, bf16[1,1,512,128]{3,2,1,0:T(8,128)(2,1)}, u32[]{:S(2)}) copy-start(bf16[1,1,512,128]{3,2,1,0:T(8,128)(2,1)} %param.16) | copy-start | bytes 393220
  6.5 16.4 %copy-start.3 = (bf16[1,4,512]{2,1,0:T(4,128)(2,1)S(1)}, bf16[1,4,512]{2,1,0:T(4,128)(2,1)}, u32[]{:S(2)}) copy-start(bf16[1,4,512]{2,1,0:T(4,128)(2,1)} %param.19) | copy-start | bytes 12292
  6.5 24.6 %copy-start.5 = (s32[1,10]{1,0:T(1,128)S(1)}, s32[1,10]{1,0:T(1,128)}, u32[]{:S(2)}) copy-start(s32[1,10]{1,0:T(1,128)} %param.20) | copy-start | bytes 124
  10.5 14.8 %all-to-all-start.2 = ((bf16[16,4,32]{2,1,0:T(4,128)(2,1)}), bf16[16,4,32]{2,1,0:T(4,128)(2,1)S(1)}, u32[]{:S(2)}, u32[]{:S(2)}) async-start(bf16[16,4,32]{2,1,0:T(4,128)(2,1)} %copy.68), calls=%async_computation.2 | async-start | bytes 32768 | tf_op jit(solution)/shard_map/all_to_all | solution.py:122
  17.7 15.4 %copy-start.2 = (s32[1,256]{1,0:T(1,128)S(1)}, s32[1,256]{1,0:T(1,128)}, u32[]{:S(2)}) copy-start(s32[1,256]{1,0:T(1,128)} %param.21) | copy-start | bytes 3076
  25.3 13.6 %all-to-all-start.5 = ((bf16[16,4,32]{2,1,0:T(4,128)(2,1)}), bf16[16,4,32]{2,1,0:T(4,128)(2,1)S(1)}, u32[]{:S(2)}, u32[]{:S(2)}) async-start(bf16[16,4,32]{2,1,0:T(4,128)(2,1)} %copy.73), calls=%async_computation.5 | async-start | bytes 32768 | tf_op jit(solution)/shard_map/all_to_all | solution.py:123
  38.9 23.3 %all-to-all-start = ((bf16[16,4,4096]{2,1,0:T(4,128)(2,1)}), bf16[16,4,4096]{2,1,0:T(4,128)(2,1)S(1)}, u32[]{:S(2)}, u32[]{:S(2)}) async-start(bf16[16,4,4096]{2,1,0:T(4,128)(2,1)} %copy.65), calls=%async_computation | async-start | bytes 1048576 | tf_op jit(solution)/shard_map/all_to_all | solution.py:118
  62.2 22.0 %all-to-all-start.3 = ((bf16[16,4,4096]{2,1,0:T(4,128)(2,1)}), bf16[16,4,4096]{2,1,0:T(4,128)(2,1)S(1)}, u32[]{:S(2)}, u32[]{:S(2)}) async-start(bf16[16,4,4096]{2,1,0:T(4,128)(2,1)} %copy.70), calls=%async_computation.3 | async-start | bytes 1048576 | tf_op jit(solution)/shard_map/all_to_all | solution.py:119
  66.7 14.2 %collective-permute-start.3 = (bf16[4,512]{1,0:T(4,128)(2,1)S(1)}, bf16[4,512]{1,0:T(4,128)(2,1)S(1)}, u32[]{:S(2)}, u32[]{:S(2)}) collective-permute-start(bf16[4,512]{1,0:T(4,128)(2,1)S(1)} %squeeze_reshape.6), channel_id=1, source_target_pairs={{8,0},{12,4},{16,8},{20,12},{24,16},{28,20},{32,24},{36,28},{40,32... | collective-permute-start | bytes 12296 | tf_op jit(solution)/shard_map/ppermute | solution.py:17
  68.0 13.0 %collective-permute-start.2 = (bf16[4,512]{1,0:T(4,128)(2,1)S(1)}, bf16[4,512]{1,0:T(4,128)(2,1)S(1)}, u32[]{:S(2)}, u32[]{:S(2)}) collective-permute-start(bf16[4,512]{1,0:T(4,128)(2,1)S(1)} %squeeze_reshape.6), channel_id=1, source_target_pairs={{4,0},{8,4},{12,8},{16,12},{20,16},{24,20},{28,24},{32,28},{36,32}... | collective-permute-start | bytes 12296 | tf_op jit(solution)/shard_map/ppermute | solution.py:17
  69.6 48.7 %collective-permute-start.7 = (bf16[4,512]{1,0:T(4,128)(2,1)S(1)}, bf16[4,512]{1,0:T(4,128)(2,1)S(1)}, u32[]{:S(2)}, u32[]{:S(2)}) collective-permute-start(bf16[4,512]{1,0:T(4,128)(2,1)S(1)} %squeeze_reshape.7), channel_id=1, source_target_pairs={{8,0},{12,4},{16,8},{20,12},{24,16},{28,20},{32,24},{36,28},{40,32... | collective-permute-start | bytes 12296 | tf_op jit(solution)/shard_map/ppermute | solution.py:17
  70.8 48.8 %collective-permute-start.6 = (bf16[4,512]{1,0:T(4,128)(2,1)S(1)}, bf16[4,512]{1,0:T(4,128)(2,1)S(1)}, u32[]{:S(2)}, u32[]{:S(2)}) collective-permute-start(bf16[4,512]{1,0:T(4,128)(2,1)S(1)} %squeeze_reshape.7), channel_id=1, source_target_pairs={{4,0},{8,4},{12,8},{16,12},{20,16},{24,20},{28,24},{32,28},{36,32}... | collective-permute-start | bytes 12296 | tf_op jit(solution)/shard_map/ppermute | solution.py:17
  81.6 45.9 %collective-permute-start.1 = (bf16[4,512,128]{2,1,0:T(8,128)(2,1)S(1)}, bf16[4,512,128]{2,1,0:T(8,128)(2,1)S(1)}, u32[]{:S(2)}, u32[]{:S(2)}) collective-permute-start(bf16[4,512,128]{2,1,0:T(8,128)(2,1)S(1)} %reshape.367), channel_id=1, source_target_pairs={{8,0},{12,4},{16,8},{20,12},{24,16},{28,20},{32,24},{36,28},{40,32... | collective-permute-start | bytes 1572872 | tf_op jit(solution)/shard_map/ppermute | solution.py:17
  82.9 44.6 %collective-permute-start = (bf16[4,512,128]{2,1,0:T(8,128)(2,1)S(1)}, bf16[4,512,128]{2,1,0:T(8,128)(2,1)}, u32[]{:S(2)}, u32[]{:S(2)}) collective-permute-start(bf16[4,512,128]{2,1,0:T(8,128)(2,1)S(1)} %reshape.367), channel_id=1, source_target_pairs={{4,0},{8,4},{12,8},{16,12},{20,16},{24,20},{28,24},{32,28},{36,32}... | collective-permute-start | bytes 1572872 | tf_op jit(solution)/shard_map/ppermute | solution.py:17
  84.2 28.4 %all-to-all-start.1 = ((bf16[16,2,2048]{2,1,0:T(2,128)(2,1)}), bf16[16,2,2048]{2,1,0:T(2,128)(2,1)S(1)}, u32[]{:S(2)}, u32[]{:S(2)}) async-start(bf16[16,2,2048]{2,1,0:T(2,128)(2,1)} %reshape.407), calls=%async_computation.1 | async-start | bytes 262144 | tf_op jit(solution)/shard_map/all_to_all | solution.py:120
  94.8 35.1 %collective-permute-start.5 = (bf16[4,512,128]{2,1,0:T(8,128)(2,1)S(1)}, bf16[4,512,128]{2,1,0:T(8,128)(2,1)}, u32[]{:S(2)}, u32[]{:S(2)}) collective-permute-start(bf16[4,512,128]{2,1,0:T(8,128)(2,1)S(1)} %reshape.371), channel_id=1, source_target_pairs={{8,0},{12,4},{16,8},{20,12},{24,16},{28,20},{32,24},{36,28},{40,32... | collective-permute-start | bytes 1572872 | tf_op jit(solution)/shard_map/ppermute | solution.py:17
  112.6 14.4 %all-to-all-start.4 = ((bf16[16,2,2048]{2,1,0:T(2,128)(2,1)}), bf16[16,2,2048]{2,1,0:T(2,128)(2,1)S(1)}, u32[]{:S(2)}, u32[]{:S(2)}) async-start(bf16[16,2,2048]{2,1,0:T(2,128)(2,1)} %reshape.409), calls=%async_computation.4 | async-start | bytes 262144 | tf_op jit(solution)/shard_map/all_to_all | solution.py:121
  118.3 11.6 %collective-permute-start.4 = (bf16[4,512,128]{2,1,0:T(8,128)(2,1)S(1)}, bf16[4,512,128]{2,1,0:T(8,128)(2,1)}, u32[]{:S(2)}, u32[]{:S(2)}) collective-permute-start(bf16[4,512,128]{2,1,0:T(8,128)(2,1)S(1)} %reshape.371), channel_id=1, source_target_pairs={{4,0},{8,4},{12,8},{16,12},{20,16},{24,20},{28,24},{32,28},{36,32}... | collective-permute-start | bytes 1572872 | tf_op jit(solution)/shard_map/ppermute | solution.py:17
  175.7 8.6 %copy-start = (bf16[1,512,1024]{2,1,0:T(8,128)(2,1)S(1)}, bf16[1,512,1024]{2,1,0:T(8,128)(2,1)}, u32[]{:S(2)}) copy-start(bf16[1,512,1024]{2,1,0:T(8,128)(2,1)} %param.13) | copy-start | bytes 3145732
  178.3 17.2 %all-to-all-start.6 = ((bf16[16,2,4096]{2,1,0:T(2,128)(2,1)}), bf16[16,2,4096]{2,1,0:T(2,128)(2,1)S(1)}, u32[]{:S(2)}, u32[]{:S(2)}) async-start(bf16[16,2,4096]{2,1,0:T(2,128)(2,1)} %reshape.411), calls=%async_computation.6 | async-start | bytes 524288 | tf_op jit(solution)/shard_map/all_to_all | solution.py:190
  197.8 55.2 %all-to-all-start.7 = ((bf16[4,1,512,1024]{2,3,1,0:T(8,128)(2,1)}), bf16[4,1,512,1024]{2,3,1,0:T(8,128)(2,1)}, u32[]{:S(2)}, u32[]{:S(2)}) async-start(bf16[4,1,512,1024]{2,3,1,0:T(8,128)(2,1)} %stack.22), calls=%async_computation.7 | async-start | bytes 8388608 | tf_op jit(solution)/shard_map/all_to_all | solution.py:197
  301.4 6.0 %copy-start.4 = (s32[2,128]{1,0:T(2,128)S(1)}, s32[2,128]{1,0:T(2,128)}, u32[]{:S(2)}) copy-start(s32[2,128]{1,0:T(2,128)} %param.22) | copy-start | bytes 3076
  301.4 6.0 %copy-start.6 = (s32[1,2]{1,0:T(1,128)S(1)}, s32[1,2]{1,0:T(1,128)}, u32[]{:S(2)}) copy-start(s32[1,2]{1,0:T(1,128)} %param.23) | copy-start | bytes 28
  301.4 118.6 %all-to-all-start.8 = ((bf16[16,2,65536]{2,1,0:T(2,128)(2,1)}), bf16[16,2,65536]{2,1,0:T(2,128)(2,1)}, u32[]{:S(2)}, u32[]{:S(2)}) async-start(bf16[16,2,65536]{2,1,0:T(2,128)(2,1)} %reshape.405), calls=%async_computation.8 | async-start | bytes 8388608 | tf_op jit(solution)/shard_map/all_to_all | solution.py:199
  306.1 139.2 %all-gather.2.cloned.1.call-start = ((), (), s32[]{:S(2)}) async-start(), calls=%async_computation.10 | async-start | bytes 4456448 | tf_op jit(solution)/shard_map/all_gather | solution.py:204
Sparse Core Ops, SparseCore 0:
  309.1 108.4 all-gather.1
